TPU v7x, 256 devices: a whole 4x4x8 slice. The times are simulated.
256 devices in a mesh: dom: 32 (over x, y, core), pair: 8 (over z).
Axes of the slice: x: 4, y: 4, z: 8, core: 2. Of those that a mesh axis runs over, the one named last changes fastest.
Arguments:
- occupied: bfloat16 [12, 128, 256, 128], P(None, 'dom'), may hold values from -6 to 6
- virtual: bfloat16 [12, 128, 256, 128], P(None, 'dom'), may hold values from -6 to 6
- pair_ids: int32 [32, 2], P('pair'), may hold values from 0 to 11
Outputs:
- potentials: bfloat16 [32, 128, 256, 128], P('pair', 'dom')
- panel: float32 [32, 32], P('dom', 'pair')
Inputs may be any that keep to these rules, and one draw needn't show every extreme that they name: `pair_ids`: each row holds an occupied orbital's index and a virtual orbital's index.
All inputs are finite; a program needn't handle non-finite values.
Results may differ from a plain program's by a relative error of at most 0.001.
Values may be sent and summed in bfloat16 or wider, within the bound.
A program may use at most 128 MiB of HBM per device.

v0:
```python
import functools
import math

import jax
import jax.numpy as jnp
import numpy as np
from jax import lax
from jax.experimental import pallas as pl
from jax.experimental.pallas import tpu as pltpu
from jax.sharding import PartitionSpec as P

MESH = pl.DeviceIdType.MESH
f32 = jnp.float32
bf16 = jnp.bfloat16

w = 0.8 / 6.0
keep = 1.0 - 0.8


def lanes_of(shape):
    return lax.broadcasted_iota(jnp.int32, shape, len(shape) - 1)


def turn(value, amount):
    return pltpu.roll(value, amount % 128, value.ndim - 1)


def beside_z(value, step):
    lane = lanes_of(value.shape)
    low = jnp.where(lane >= step, turn(value, step), 0.0)
    high = jnp.where(lane < 128 - step, turn(value, -step), 0.0)
    return low + high


def plane_sum(ref, at, first, rows, step):
    middle = ref[at + (pl.ds(first + 8, rows),)]
    above = ref[at + (pl.ds(first + 7, rows),)]
    below = ref[at + (pl.ds(first + 9, rows),)]
    return middle, above + below + beside_z(middle, step)


def fold_rows(sums, mixed, at, rows):
    even = sums[at + (pl.ds(8, rows, stride=2),)]
    odd = sums[at + (pl.ds(9, rows, stride=2),)]
    before = sums[at + (pl.ds(7, rows, stride=2),)]
    after = sums[at + (pl.ds(10, rows, stride=2),)]
    folded = even + odd
    weighted = mixed[at + (pl.ds(8, rows, stride=2),)] + mixed[at + (pl.ds(9, rows, stride=2),)]
    return folded, weighted + w * (folded + before + after)


def fold_lanes(folded, weighted, step, upper):
    lane = lanes_of(folded.shape)
    if upper:
        total = weighted + turn(weighted, step)
        low, high = turn(folded, 2 * step), turn(folded, -step)
    else:
        total = weighted + turn(weighted, -step)
        low, high = turn(folded, step), turn(folded, -2 * step)
    low = jnp.where(lane >= 2 * step, low, 0.0)
    high = jnp.where(lane < 128 - 2 * step, high, 0.0)
    return 0.5 * (total + w * (low + high))


def zero_rows(ref, lead, total):
    zeros = jnp.zeros((8, 128), f32)
    for at in np.ndindex(*lead):
        ref[at + (pl.ds(0, 8),)] = zeros
        ref[at + (pl.ds(total - 8, 8),)] = zeros


def kernel(n, groups, ids_ref, occ, vir, sy_ref, sz_ref, diag_ref, pot_ref, panel_ref,
           F, Z, Y, S0, M0, X1, FC, H, Z1, V1, S1, M1, SPEC, REC, D, INV, UP, REC2, WB, U5,
           CL, CR, F16, HL, HR, X16, BL, BR, PART, REC3, IDV, IDR, IDS,
           s1, r1, s2, r2, s3, r3, s_id, r_id, s_h, r_h, loc):
    me = lax.axis_index("dom")
    group = lax.axis_index("pair")
    barrier = pltpu.get_barrier_semaphore()

    def dom_at(i):
        return lax.rem(me + i, n)

    def pair_at(i):
        return lax.rem(group + i, groups)

    def signal_dom(i, carry):
        pl.semaphore_signal(barrier, inc=1, device_id={"dom": dom_at(i)}, device_id_type=MESH)
        return carry

    def signal_pair(i, carry):
        pl.semaphore_signal(barrier, inc=1, device_id={"pair": pair_at(i)}, device_id_type=MESH)
        return carry

    lax.fori_loop(1, n, signal_dom, 0)
    lax.fori_loop(1, groups, signal_pair, 0)

    first, last = me == 0, me == n - 1
    inner_l, inner_r = me > 0, me < n - 1
    mask_l = jnp.where(inner_l, 1.0, 0.0).astype(f32)
    mask_r = jnp.where(inner_r, 1.0, 0.0).astype(f32)

    zero_rows(F, (10, 4), 272)
    zero_rows(Z, (6, 4), 272)
    zero_rows(Y, (8, 4), 272)
    zero_rows(S0, (4,), 272)
    zero_rows(X1, (10, 2), 144)
    zero_rows(FC, (4, 2), 144)
    zero_rows(H, (8, 2), 144)
    zero_rows(Z1, (6, 2), 144)
    zero_rows(S1, (2,), 144)
    UP[pl.ds(0, 2)] = jnp.zeros((2, 2, 128), f32)
    UP[pl.ds(n + 2, 2)] = jnp.zeros((2, 2, 128), f32)
    REC[pl.ds(0, 2)] = jnp.zeros((2, 10, 128), f32)
    REC[pl.ds(n + 2, 2)] = jnp.zeros((2, 10, 128), f32)

    @pl.when(first)
    def _():
        F[2] = jnp.zeros((4, 272, 128), f32)
        HL[...] = jnp.zeros((2, 4, 256, 128), bf16)
        CL[...] = jnp.zeros((2, 128, 128), f32)
        X1[pl.ds(2, 2)] = jnp.zeros((2, 2, 144, 128), f32)

    @pl.when(last)
    def _():
        F[7] = jnp.zeros((4, 272, 128), f32)
        HR[...] = jnp.zeros((2, 4, 256, 128), bf16)
        CR[...] = jnp.zeros((2, 128, 128), f32)
        X1[pl.ds(6, 2)] = jnp.zeros((2, 2, 144, 128), f32)

    @pl.when(me < 2)
    def _():
        BL[...] = jnp.zeros((2, 2, 128, 128), bf16)

    @pl.when(me > n - 3)
    def _():
        BR[...] = jnp.zeros((2, 2, 128, 128), bf16)

    row = lax.broadcasted_iota(jnp.int32, (8, 128), 0)
    col = lax.broadcasted_iota(jnp.int32, (8, 128), 1)
    own_ids = jnp.zeros((8, 128), jnp.int32)
    for i in range(4):
        for c in range(2):
            own_ids = jnp.where((row == i) & (col == c), ids_ref[i, c], own_ids)
    IDV[...] = own_ids
    IDR[group] = own_ids

    for p in range(4):
        io, iv = ids_ref[p, 0], ids_ref[p, 1]

        def density(x, carry, p=p, io=io, iv=iv):
            rho = occ[io, x].astype(f32) * vir[iv, x].astype(f32)
            F[x + 3, p, pl.ds(8, 256)] = rho
            return carry

        lax.fori_loop(0, 4, density, 0)
        for x in (1, 2):
            F16[x - 1, p] = F[x + 3, p, pl.ds(8, 256)].astype(bf16)

    def own_sweep(p, carry):
        for r in (0, 128):
            for x in range(4):
                middle, sides = plane_sum(F, (x + 3, p), r, 128, 1)
                if x > 0:
                    sides = sides + F[x + 2, p, pl.ds(r + 8, 128)]
                if x < 3:
                    sides = sides + F[x + 4, p, pl.ds(r + 8, 128)]
                Z[x + 1, p, pl.ds(r + 8, 128)] = keep * middle + w * sides
            Z[0, p, pl.ds(r + 8, 128)] = (mask_l * w) * F[3, p, pl.ds(r + 8, 128)]
            Z[5, p, pl.ds(r + 8, 128)] = (mask_r * w) * F[6, p, pl.ds(r + 8, 128)]
        return carry

    lax.fori_loop(0, 4, own_sweep, 0)

    for q in range(-1, 3):
        def fold0(p, carry, q=q):
            for r in (0, 128):
                at = pl.ds(r + 8, 128)
                if q == -1:
                    s, far = Z[0, p, at], Z[1, p, at]
                elif q == 2:
                    s, far = Z[5, p, at], Z[4, p, at]
                else:
                    s = Z[2 * q + 1, p, at] + Z[2 * q + 2, p, at]
                    far = Z[2 * q, p, at] + Z[2 * q + 3, p, at]
                S0[p, at] = s
                M0[p, at] = (keep + 2.0 * w) * s + w * far
            return carry

        lax.fori_loop(0, 4, fold0, 0)
        for ph in range(2):
            low = fold_lanes(*fold_rows(S0, M0, (2 * ph,), 128), 1, False)
            high = fold_lanes(*fold_rows(S0, M0, (2 * ph + 1,), 128), 1, True)
            value = jnp.where(lanes_of(low.shape) % 2 == 0, low, high)
            if q == -1:
                value = value * mask_l
            if q == 2:
                value = value * mask_r
            FC[q + 1, ph, pl.ds(8, 128)] = value

    for ph in range(2):
        at = pl.ds(8, 128)
        H[1, ph, at] = (mask_l * w) * FC[0, ph, at]
        H[6, ph, at] = (mask_r * w) * FC[3, ph, at]
        for i in range(-1, 3):
            middle, sides = plane_sum(FC, (i + 1, ph), 0, 128, 2)
            if i > -1:
                sides = sides + FC[i, ph, at]
            if i < 2:
                sides = sides + FC[i + 2, ph, at]
            value = keep * middle + w * sides
            if i == -1:
                value = value * mask_l
            if i == 2:
                value = value * mask_r
            H[i + 3, ph, at] = value

    parts = []
    for q in range(-2, 3):
        for ph in range(2):
            at = pl.ds(8, 128)
            lo, hi = 2 * q, 2 * q + 1
            pick = lambda i: H[i + 3, ph, at] if -2 <= i <= 3 else None
            both = [v for v in (pick(lo), pick(hi)) if v is not None]
            ends = [v for v in (pick(lo - 1), pick(hi + 1)) if v is not None]
            s = sum(both[1:], both[0]) if both else jnp.zeros((128, 128), f32)
            far = sum(ends[1:], ends[0])
            S1[ph, at] = s
            M1[ph, at] = (keep + 2.0 * w) * s + w * far
        low = fold_lanes(*fold_rows(S1, M1, (0,), 64), 2, False)
        high = fold_lanes(*fold_rows(S1, M1, (1,), 64), 2, True)
        parts.append(jnp.where(lanes_of(low.shape) % 4 < 2, low, high))
    sy, sz = sy_ref[...], sz_ref[...]
    highest = lax.Precision.HIGHEST
    wide = jnp.dot(sy, jnp.concatenate(parts, 1), precision=highest, preferred_element_type=f32)
    tall = jnp.concatenate([wide[:, 128 * j: 128 * j + 128] for j in range(5)], 0)
    WB[...] = jnp.dot(tall, sz, precision=highest, preferred_element_type=f32)
    for d in range(n):
        for j in range(5):
            SPEC[d, pl.ds(2 * j, 2)] = WB[pl.ds(64 * j + 2 * d, 2)]
    REC[me + 2] = SPEC[me]

    pl.semaphore_wait(barrier, n - 1 + groups - 1)

    def remote(src, dst, send, recv, where):
        return pltpu.make_async_remote_copy(
            src_ref=src, dst_ref=dst, send_sem=send, recv_sem=recv, device_id=where, device_id_type=MESH
        )

    def go1(t):
        return remote(SPEC.at[t], REC.at[me + 2], s1.at[t], r1.at[me], {"dom": t})

    def come1(s):
        return remote(SPEC.at[s], REC.at[s + 2], s1.at[s], r1.at[s], {"dom": s})

    def go2(t):
        return remote(UP.at[pl.ds(t, 5)], REC2.at[me], s2.at[t], r2.at[me], {"dom": t})

    def come2(s):
        return remote(UP.at[pl.ds(s, 5)], REC2.at[s], s2.at[s], r2.at[s], {"dom": s})

    def go3(t):
        return remote(PART.at[t], REC3.at[me], s3.at[t], r3.at[me], {"dom": t})

    def come3(s):
        return remote(PART.at[s], REC3.at[s], s3.at[s], r3.at[s], {"dom": s})

    def go_id(t):
        return remote(IDV, IDR.at[group], s_id.at[t], r_id.at[group], {"pair": t})

    def come_id(s):
        return remote(IDV, IDR.at[s], s_id.at[s], r_id.at[s], {"pair": s})

    def each(count, at, build, what):
        def body(i, carry):
            getattr(build(at(i)), what)()
            return carry

        lax.fori_loop(1, count, body, 0)

    each(n, dom_at, go1, "start")
    each(groups, pair_at, go_id, "start")

    in0, in1 = pl.ds(8, 256), pl.ds(8, 128)
    halos = [
        (FC.at[3, :, in1], CL, 1),
        (FC.at[0, :, in1], CR, -1),
        (F.at[6, :, in0], F.at[2, :, in0], 1),
        (F.at[3, :, in0], F.at[7, :, in0], -1),
        (X1.at[pl.ds(4, 2), :, in1], X1.at[pl.ds(2, 2), :, in1], 1),
        (X1.at[pl.ds(4, 2), :, in1], X1.at[pl.ds(6, 2), :, in1], -1),
        (X16, BL, 2),
        (X16, BR, -2),
        (F16, HL, 1),
        (F16, HR, -1),
    ]

    def halo(k, what):
        src, dst, off = halos[k]
        outgoing = what in ("start", "wait_send")
        towards = off if outgoing else -off
        there = (me < n - towards) if towards > 0 else (me >= -towards)

        @pl.when(there)
        def _():
            copy = remote(src, dst, s_h.at[k], r_h.at[k], {"dom": lax.rem(me + off + n, n)})
            getattr(copy, what)()

    halo(0, "start")
    halo(1, "start")

    base = diag_ref[me]

    def pivot(x, before):
        value = 1.0 / (base - before)
        INV[x] = value
        return value

    lax.fori_loop(0, n, pivot, jnp.zeros((2, 128), f32))

    halo(0, "wait_recv")
    halo(1, "wait_recv")
    for ph in range(2):
        for i, side in ((0, CL), (1, CR)):
            value = FC[i + 1, ph, in1] + side[ph]
            X1[i + 4, ph, in1] = value
            X16[i, ph] = value.astype(bf16)
    for k in (4, 5, 6, 7, 2, 3, 8, 9):
        halo(k, "start")

    each(n, dom_at, come1, "wait_recv")

    def forward(x, before):
        value = before
        for j in range(5):
            value = value + REC[x + 4 - j, pl.ds(2 * j, 2)]
        value = value * INV[x]
        D[x] = value
        return value

    lax.fori_loop(0, n, forward, jnp.zeros((2, 128), f32))

    def backward(i, after):
        x = n - 1 - i
        value = D[x] + INV[x] * after
        UP[x + 2] = value
        return value

    lax.fori_loop(0, n, backward, jnp.zeros((2, 128), f32))
    REC2[me] = UP[pl.ds(me, 5)]
    each(n, dom_at, go2, "start")

    for k in (2, 3, 8, 9):
        halo(k, "wait_recv")

    def widen(p, carry):
        for x in range(2):
            F[x, p, in0] = HL[x, p].astype(f32)
            F[x + 8, p, in0] = HR[x, p].astype(f32)
        return carry

    lax.fori_loop(0, 4, widen, 0)

    def mask0(x):
        at = 4 * me + x
        return jnp.where((at >= 0) & (at < 4 * n), 1.0, 0.0).astype(f32)

    def sweep_y(i, carry):
        x, p = i // 4 - 2, lax.rem(i, 4)
        for r in (0, 128):
            at = pl.ds(r + 8, 128)
            middle, sides = plane_sum(F, (x + 3, p), r, 128, 1)
            sides = sides + F[x + 2, p, at] + F[x + 4, p, at]
            Y[x + 2, p, at] = (w * (1.0 + keep)) * middle + (w * w) * sides
        return carry

    lax.fori_loop(0, 32, sweep_y, 0)

    for k in (4, 5, 6, 7):
        halo(k, "wait_recv")
    for i in range(2):
        for ph in range(2):
            X1[i, ph, in1] = BL[i, ph].astype(f32)
            X1[i + 8, ph, in1] = BR[i, ph].astype(f32)

    each(n, dom_at, come2, "wait_recv")
    for d in range(n):
        for j in range(5):
            WB[pl.ds(64 * j + 2 * d, 2)] = REC2[d, j]
    tall = jnp.dot(WB[...], sz, precision=highest, preferred_element_type=f32)
    wide = jnp.concatenate([tall[64 * j: 64 * j + 64] for j in range(5)], 1)
    wide = jnp.dot(sy, wide, precision=highest, preferred_element_type=f32)
    for j in range(5):
        U5[j] = wide[:, 128 * j: 128 * j + 128]

    def mask1(i):
        at = 2 * me + i
        return jnp.where((at >= 0) & (at < 2 * n), 1.0, 0.0).astype(f32)

    for ph in range(2):
        for i in range(-3, 5):
            middle, sides = plane_sum(X1, (i + 4, ph), 0, 128, 2)
            sides = sides + X1[i + 3, ph, in1] + X1[i + 5, ph, in1]
            H[i + 3, ph, in1] = (w * (1.0 + keep)) * middle + (w * w) * sides
        for j in range(-2, 3):
            u = U5[j + 2]
            lane = lanes_of(u.shape)
            if ph == 0:
                spread = jnp.where(lane % 4 < 2, u, turn(u, 2))
            else:
                spread = jnp.where(lane % 4 < 2, turn(u, -2), u)
            for i in (2 * j, 2 * j + 1):
                if -3 <= i < 5:
                    for odd in (8, 9):
                        at = pl.ds(odd, 64, stride=2)
                        H[i + 3, ph, at] = H[i + 3, ph, at] + spread
        for i in (-3, -2, -1, 2, 3, 4):
            H[i + 3, ph, in1] = H[i + 3, ph, in1] * mask1(i)
        for i in range(-2, 4):
            middle, sides = plane_sum(H, (i + 3, ph), 0, 128, 2)
            sides = sides + H[i + 2, ph, in1] + H[i + 4, ph, in1]
            value = keep * middle + w * (sides + X1[i + 4, ph, in1])
            Z1[i + 2, ph, in1] = value * mask1(i)
        for i in range(-1, 3):
            middle, sides = plane_sum(Z1, (i + 2, ph), 0, 128, 2)
            sides = sides + Z1[i + 1, ph, in1] + Z1[i + 3, ph, in1]
            value = keep * middle + w * (sides + X1[i + 4, ph, in1])
            V1[i + 1, ph] = value * mask1(i)

    def add_coarse(j, carry):
        for p in range(4):
            for r in (0, 64):
                v = V1[j, p // 2, pl.ds(r, 64)]
                even = lanes_of(v.shape) % 2 == 0
                if p % 2 == 0:
                    spread = jnp.where(even, v, turn(v, 1))
                else:
                    spread = jnp.where(even, turn(v, -1), v)
                for x in range(2):
                    for odd in (8, 9):
                        at = pl.ds(2 * r + odd, 64, stride=2)
                        Y[2 * j + x, p, at] = Y[2 * j + x, p, at] + spread
        return carry

    lax.fori_loop(0, 4, add_coarse, 0)

    @pl.when(first)
    def _():
        Y[pl.ds(0, 2)] = jnp.zeros((2, 4, 272, 128), f32)

    @pl.when(last)
    def _():
        Y[pl.ds(6, 2)] = jnp.zeros((2, 4, 272, 128), f32)

    def sweep_z(i, carry):
        x, p = i // 4 - 1, lax.rem(i, 4)
        mask = mask0(x)
        for r in (0, 128):
            at = pl.ds(r + 8, 128)
            middle, sides = plane_sum(Y, (x + 2, p), r, 128, 1)
            sides = sides + Y[x + 1, p, at] + Y[x + 3, p, at]
            Z[x + 1, p, at] = (keep * middle + w * (sides + F[x + 3, p, at])) * mask
        return carry

    lax.fori_loop(0, 24, sweep_z, 0)

    def sweep_out(i, carry):
        x, p = i // 4, lax.rem(i, 4)
        for r in (0, 128):
            at = pl.ds(r + 8, 128)
            middle, sides = plane_sum(Z, (x + 1, p), r, 128, 1)
            sides = sides + Z[x, p, at] + Z[x + 2, p, at]
            value = keep * middle + w * (sides + F[x + 3, p, at])
            pot_ref[p, x, pl.ds(r, 128)] = value.astype(bf16)
        return carry

    lax.fori_loop(0, 16, sweep_out, 0)

    each(groups, pair_at, come_id, "wait_recv")
    copy = pltpu.make_async_copy(IDR, IDS, loc)
    copy.start()
    copy.wait()

    def panel_rows(g, carry):
        at_o = [IDS[g, i, 0] for i in range(4)]
        at_v = [IDS[g, i, 1] for i in range(4)]

        def cells(c, sums):
            x, r = c // 8, lax.rem(c, 8) * 32
            at = pl.ds(pl.multiple_of(r, 32), 32)
            pots = [pot_ref[q, x, at].astype(f32) for q in range(4)]
            new = []
            for i in range(4):
                rho = (occ[at_o[i], x, at] * vir[at_v[i], x, at]).astype(f32)
                for q in range(4):
                    product = rho * pots[q]
                    new.append(sums[4 * i + q] + jnp.sum(product.reshape(4, 8, 128), 0))
            return tuple(new)

        sums = lax.fori_loop(0, 32, cells, tuple(jnp.zeros((8, 128), f32) for _ in range(16)))
        for i in range(4):
            rows = [jnp.sum(sums[4 * i + q], 0, keepdims=True) for q in range(4)]
            PART[4 * g + i] = jnp.concatenate(rows, 0)
        return carry

    lax.fori_loop(0, groups, panel_rows, 0)
    REC3[me] = PART[me]
    each(n, dom_at, go3, "start")
    each(n, dom_at, come3, "wait_recv")
    total = lax.fori_loop(0, n, lambda s, t: t + REC3[s], jnp.zeros((4, 128), f32))
    total = jnp.concatenate([total, jnp.zeros((4, 128), f32)], 0)
    row_sums = lax.dot_general(
        jnp.ones((8, 128), f32), total, (((1,), (1,)), ((), ())), precision=highest, preferred_element_type=f32
    )
    panel_ref[...] = row_sums[0:1, 0:4] / float(4 * 256 * 128 * n)

    for k in range(len(halos)):
        halo(k, "wait_send")
    each(n, dom_at, go1, "wait_send")
    each(n, dom_at, go2, "wait_send")
    each(n, dom_at, go3, "wait_send")
    each(groups, pair_at, go_id, "wait_send")


def tables():
    def sines(length):
        steps = np.arange(length, dtype=np.float64) + 1.0
        return np.sqrt(2.0 / (length + 1)) * np.sin(math.pi * steps[:, None] * steps[None, :] / (length + 1))

    def lams(length):
        return 2.0 - 2.0 * np.cos(math.pi * (np.arange(length, dtype=np.float64) + 1.0) / (length + 1))

    sy = sines(64).astype(np.float32)
    sz = np.kron(sines(32), np.eye(4)).astype(np.float32)
    diag = 2.0 + lams(64)[:, None] + np.repeat(lams(32), 4)[None, :]
    return sy, sz, diag.astype(np.float32).reshape(32, 2, 128)


def solution(mesh):
    n, groups = mesh.shape["dom"], mesh.shape["pair"]
    sy, sz, diag = tables()
    dma, vm = pltpu.SemaphoreType.DMA, pltpu.VMEM
    whole = pl.BlockSpec(memory_space=pltpu.VMEM)

    def shards(occupied, virtual, pair_ids):
        return pl.pallas_call(
            functools.partial(kernel, n, groups),
            out_shape=(
                jax.ShapeDtypeStruct((4, 4, 256, 128), bf16),
                jax.ShapeDtypeStruct((1, 4), f32),
            ),
            in_specs=[pl.BlockSpec(memory_space=pltpu.SMEM)] + [whole] * 5,
            out_specs=(whole, whole),
            scratch_shapes=[
                vm((10, 4, 272, 128), f32),
                vm((6, 4, 272, 128), f32),
                vm((8, 4, 272, 128), f32),
                vm((4, 272, 128), f32),
                vm((4, 272, 128), f32),
                vm((10, 2, 144, 128), f32),
                vm((4, 2, 144, 128), f32),
                vm((8, 2, 144, 128), f32),
                vm((6, 2, 144, 128), f32),
                vm((4, 2, 128, 128), f32),
                vm((2, 144, 128), f32),
                vm((2, 144, 128), f32),
                vm((n, 10, 128), f32),
                vm((n + 4, 10, 128), f32),
                vm((n, 2, 128), f32),
                vm((n, 2, 128), f32),
                vm((n + 4, 2, 128), f32),
                vm((n, 5, 2, 128), f32),
                vm((320, 128), f32),
                vm((5, 64, 128), f32),
                vm((2, 128, 128), f32),
                vm((2, 128, 128), f32),
                vm((2, 4, 256, 128), bf16),
                vm((2, 4, 256, 128), bf16),
                vm((2, 4, 256, 128), bf16),
                vm((2, 2, 128, 128), bf16),
                vm((2, 2, 128, 128), bf16),
                vm((2, 2, 128, 128), bf16),
                vm((n, 4, 128), f32),
                vm((n, 4, 128), f32),
                vm((8, 128), jnp.int32),
                vm((groups, 8, 128), jnp.int32),
                pltpu.SMEM((groups, 8, 128), jnp.int32),
                dma((n,)), dma((n,)), dma((n,)), dma((n,)), dma((n,)), dma((n,)),
                dma((groups,)), dma((groups,)),
                dma((10,)), dma((10,)), dma(()),
            ],
            compiler_params=pltpu.CompilerParams(
                collective_id=0, has_side_effects=True, vmem_limit_bytes=56 << 20
            ),
            name="casida",
        )(pair_ids, occupied, virtual, jnp.asarray(sy), jnp.asarray(sz), jnp.asarray(diag))

    return jax.shard_map(
        shards,
        mesh=mesh,
        in_specs=(P(None, "dom", None, None), P(None, "dom", None, None), P("pair", None)),
        out_specs=(P("pair", "dom", None, None), P("dom", "pair")),
        check_vma=False,
    )
```

profile of v0, /device:TPU:1, one launch (start us, length us, event | category | flops | bytes accessed | tf_op | source)
XLA Modules:
  0.0 79.1 jit_solution(12451068930370262853)
XLA Ops:
  0.6 1.3 %copy.8.ids_ref = s32[4,2]{1,0:T(4,128)} copy(s32[4,2]{0,1:T(2,128)} %param.8) | data formatting | bytes 64 | tf_op args[2]
  2.0 73.7 %casida.1 = (bf16[4,4,256,128]{3,2,1,0:T(8,128)(2,1)}, f32[1,4]{1,0:T(1,128)}) custom-call(s32[4,2]{1,0:T(4,128)} %copy.8.ids_ref, bf16[12,4,256,128]{3,2,1,0:T(8,128)(2,1)} %occ.1, bf16[12,4,256,128]{3,2,1,0:T(8,128)(2,1)} %vir.1, f32[64,64]{1,0:T(8,128)} %constant.6.clone.sy_ref, f32[128,128]{1,0:T(8,128)} %constant.7.clone.sz_ref, ...), custom_call_target="tpu_custom_call" | custom-call | tf_op jit(solution)/shard_map/casida/pallas_call | solution.py:545
  75.7 2.3 %copy.11 = bf16[4,4,256,128]{3,2,1,0:T(8,128)(2,1)} copy(bf16[4,4,256,128]{3,2,1,0:T(8,128)(2,1)} %get-tuple-element.4) | data formatting | bytes 2097152
  78.0 1.1 %copy.12 = f32[1,4]{1,0:T(1,128)} copy(f32[1,4]{1,0:T(1,128)} %get-tuple-element.5) | data formatting | bytes 32
where the time goes:
time: 79.3 us; the launch traced here: 79.1 us
  Pallas kernels  73.7 us (93%)
  local copies, waits for them, and re-layouts  4.75 us (6%)
    pallas_call x1, Pallas kernels, shards(): pl.pallas_call(functools.partial(kernel, n, groups), out_shape=(jax.Shape...  73.7 us
    unnamed x3, local copies, waits for them, and re-layouts  4.75 us

commit v1 on v0

--- a/solution.py
+++ b/solution.py
@@ -69,10 +69,10 @@
         ref[at + (pl.ds(total - 8, 8),)] = zeros
 
 
-def kernel(n, groups, ids_ref, occ, vir, sy_ref, sz_ref, diag_ref, pot_ref, panel_ref,
-           F, Z, Y, S0, M0, X1, FC, H, Z1, V1, S1, M1, SPEC, REC, D, INV, UP, REC2, WB, U5,
-           CL, CR, F16, HL, HR, X16, BL, BR, PART, REC3, IDV, IDR, IDS,
-           s1, r1, s2, r2, s3, r3, s_id, r_id, s_h, r_h, loc):
+def kernel(n, groups, ids_hbm, occ_hbm, vir_hbm, sy_ref, sz_ref, diag_ref, pot_ref, panel_ref,
+           occ, vir, ids_ref, F, Z, Y, S0, M0, X1, FC, H, Z1, V1, S1, M1, SPEC, REC, D, INV, UP, REC2, WB, U5,
+           CL, CR, F16, HL, HR, X16, AL, AR, BL, BR, PART, REC3, IDV, IDR, IDS,
+           s1, r1, s2, r2, s3, r3, s_id, r_id, s_h, r_h, loc, in_o, in_v, in_id):
     me = lax.axis_index("dom")
     group = lax.axis_index("pair")
     barrier = pltpu.get_barrier_semaphore()
@@ -93,6 +93,15 @@
 
     lax.fori_loop(1, n, signal_dom, 0)
     lax.fori_loop(1, groups, signal_pair, 0)
+
+    ids_in = pltpu.make_async_copy(ids_hbm, ids_ref, in_id)
+    ids_in.start()
+    loads = []
+    for x in range(4):
+        loads.append(pltpu.make_async_copy(occ_hbm.at[:, x], occ.at[:, x], in_o.at[x]))
+        loads.append(pltpu.make_async_copy(vir_hbm.at[:, x], vir.at[:, x], in_v.at[x]))
+    for load in loads:
+        load.start()
 
     first, last = me == 0, me == n - 1
     inner_l, inner_r = me > 0, me < n - 1
@@ -110,22 +119,22 @@
     zero_rows(S1, (2,), 144)
     UP[pl.ds(0, 2)] = jnp.zeros((2, 2, 128), f32)
     UP[pl.ds(n + 2, 2)] = jnp.zeros((2, 2, 128), f32)
-    REC[pl.ds(0, 2)] = jnp.zeros((2, 10, 128), f32)
-    REC[pl.ds(n + 2, 2)] = jnp.zeros((2, 10, 128), f32)
+    REC[pl.ds(0, 2)] = jnp.zeros((2, 5, 2, 128), f32)
+    REC[pl.ds(n + 2, 2)] = jnp.zeros((2, 5, 2, 128), f32)
 
     @pl.when(first)
     def _():
-        F[2] = jnp.zeros((4, 272, 128), f32)
-        HL[...] = jnp.zeros((2, 4, 256, 128), bf16)
+        HL[...] = jnp.zeros((3, 4, 256, 128), bf16)
+        AL[...] = jnp.zeros((2, 128, 128), bf16)
         CL[...] = jnp.zeros((2, 128, 128), f32)
-        X1[pl.ds(2, 2)] = jnp.zeros((2, 2, 144, 128), f32)
+        X1[3] = jnp.zeros((2, 144, 128), f32)
 
     @pl.when(last)
     def _():
-        F[7] = jnp.zeros((4, 272, 128), f32)
-        HR[...] = jnp.zeros((2, 4, 256, 128), bf16)
+        HR[...] = jnp.zeros((3, 4, 256, 128), bf16)
+        AR[...] = jnp.zeros((2, 128, 128), bf16)
         CR[...] = jnp.zeros((2, 128, 128), f32)
-        X1[pl.ds(6, 2)] = jnp.zeros((2, 2, 144, 128), f32)
+        X1[6] = jnp.zeros((2, 144, 128), f32)
 
     @pl.when(me < 2)
     def _():
@@ -134,6 +143,8 @@
     @pl.when(me > n - 3)
     def _():
         BR[...] = jnp.zeros((2, 2, 128, 128), bf16)
+
+    ids_in.wait()
 
     row = lax.broadcasted_iota(jnp.int32, (8, 128), 0)
     col = lax.broadcasted_iota(jnp.int32, (8, 128), 1)
@@ -144,17 +155,93 @@
     IDV[...] = own_ids
     IDR[group] = own_ids
 
+    for load in loads:
+        load.wait()
     for p in range(4):
         io, iv = ids_ref[p, 0], ids_ref[p, 1]
 
         def density(x, carry, p=p, io=io, iv=iv):
             rho = occ[io, x].astype(f32) * vir[iv, x].astype(f32)
             F[x + 3, p, pl.ds(8, 256)] = rho
+            F16[x, p] = rho.astype(bf16)
             return carry
 
         lax.fori_loop(0, 4, density, 0)
-        for x in (1, 2):
-            F16[x - 1, p] = F[x + 3, p, pl.ds(8, 256)].astype(bf16)
+
+    pl.semaphore_wait(barrier, n - 1 + groups - 1)
+
+    def remote(src, dst, send, recv, where):
+        return pltpu.make_async_remote_copy(
+            src_ref=src, dst_ref=dst, send_sem=send, recv_sem=recv, device_id=where, device_id_type=MESH
+        )
+
+    def go1(t):
+        return remote(SPEC.at[t], REC.at[me + 2], s1, r1, {"dom": t})
+
+    others = pl.ds(0, n - 1)
+
+    def all1(what):
+        part = SPEC.at[others]
+        getattr(remote(part, part, s1, r1, {"dom": dom_at(1)}), what)()
+
+    def all2(what):
+        part = REC2.at[others]
+        getattr(remote(part, part, s2, r2, {"dom": dom_at(1)}), what)()
+
+    def all3(what):
+        part = PART.at[others]
+        getattr(remote(part, part, s3, r3, {"dom": dom_at(1)}), what)()
+
+    def go2(t):
+        return remote(UP.at[pl.ds(t, 5)], REC2.at[me], s2, r2, {"dom": t})
+
+    def go3(t):
+        return remote(PART.at[t], REC3.at[me], s3, r3, {"dom": t})
+
+    def go_id(t):
+        return remote(IDV, IDR.at[group], s_id.at[t], r_id.at[group], {"pair": t})
+
+    def come_id(s):
+        return remote(IDV, IDR.at[s], s_id.at[s], r_id.at[s], {"pair": s})
+
+    def each(count, at, build, what):
+        def body(i, carry):
+            getattr(build(at(i)), what)()
+            return carry
+
+        lax.fori_loop(1, count, body, 0)
+
+    in0, in1 = pl.ds(8, 256), pl.ds(8, 128)
+    halos = [
+        (FC.at[3, :, in1], CL, 1),
+        (FC.at[0, :, in1], CR, -1),
+        (F16.at[3], HL.at[2], 1),
+        (F16.at[0], HR.at[0], -1),
+        (F16.at[2], HL.at[1], 1),
+        (F16.at[1], HR.at[1], -1),
+        (F16.at[1], HL.at[0], 1),
+        (F16.at[2], HR.at[2], -1),
+        (X1.at[5, :, in1], X1.at[3, :, in1], 1),
+        (X1.at[4, :, in1], X1.at[6, :, in1], -1),
+        (X16.at[0], AL, 1),
+        (X16.at[1], AR, -1),
+        (X16, BL, 2),
+        (X16, BR, -2),
+    ]
+
+    def halo(k, what):
+        src, dst, off = halos[k]
+        outgoing = what in ("start", "wait_send")
+        towards = off if outgoing else -off
+        there = (me < n - towards) if towards > 0 else (me >= -towards)
+
+        @pl.when(there)
+        def _():
+            copy = remote(src, dst, s_h.at[k], r_h.at[k], {"dom": lax.rem(me + off + n, n)})
+            getattr(copy, what)()
+
+    halo(2, "start")
+    halo(3, "start")
 
     def own_sweep(p, carry):
         for r in (0, 128):
@@ -196,6 +283,9 @@
             if q == 2:
                 value = value * mask_r
             FC[q + 1, ph, pl.ds(8, 128)] = value
+
+    halo(0, "start")
+    halo(1, "start")
 
     for ph in range(2):
         at = pl.ds(8, 128)
@@ -236,77 +326,14 @@
     WB[...] = jnp.dot(tall, sz, precision=highest, preferred_element_type=f32)
     for d in range(n):
         for j in range(5):
-            SPEC[d, pl.ds(2 * j, 2)] = WB[pl.ds(64 * j + 2 * d, 2)]
+            SPEC[d, j] = WB[pl.ds(64 * j + 2 * d, 2)]
     REC[me + 2] = SPEC[me]
-
-    pl.semaphore_wait(barrier, n - 1 + groups - 1)
-
-    def remote(src, dst, send, recv, where):
-        return pltpu.make_async_remote_copy(
-            src_ref=src, dst_ref=dst, send_sem=send, recv_sem=recv, device_id=where, device_id_type=MESH
-        )
-
-    def go1(t):
-        return remote(SPEC.at[t], REC.at[me + 2], s1.at[t], r1.at[me], {"dom": t})
-
-    def come1(s):
-        return remote(SPEC.at[s], REC.at[s + 2], s1.at[s], r1.at[s], {"dom": s})
-
-    def go2(t):
-        return remote(UP.at[pl.ds(t, 5)], REC2.at[me], s2.at[t], r2.at[me], {"dom": t})
-
-    def come2(s):
-        return remote(UP.at[pl.ds(s, 5)], REC2.at[s], s2.at[s], r2.at[s], {"dom": s})
-
-    def go3(t):
-        return remote(PART.at[t], REC3.at[me], s3.at[t], r3.at[me], {"dom": t})
-
-    def come3(s):
-        return remote(PART.at[s], REC3.at[s], s3.at[s], r3.at[s], {"dom": s})
-
-    def go_id(t):
-        return remote(IDV, IDR.at[group], s_id.at[t], r_id.at[group], {"pair": t})
-
-    def come_id(s):
-        return remote(IDV, IDR.at[s], s_id.at[s], r_id.at[s], {"pair": s})
-
-    def each(count, at, build, what):
-        def body(i, carry):
-            getattr(build(at(i)), what)()
-            return carry
-
-        lax.fori_loop(1, count, body, 0)
 
     each(n, dom_at, go1, "start")
     each(groups, pair_at, go_id, "start")
 
-    in0, in1 = pl.ds(8, 256), pl.ds(8, 128)
-    halos = [
-        (FC.at[3, :, in1], CL, 1),
-        (FC.at[0, :, in1], CR, -1),
-        (F.at[6, :, in0], F.at[2, :, in0], 1),
-        (F.at[3, :, in0], F.at[7, :, in0], -1),
-        (X1.at[pl.ds(4, 2), :, in1], X1.at[pl.ds(2, 2), :, in1], 1),
-        (X1.at[pl.ds(4, 2), :, in1], X1.at[pl.ds(6, 2), :, in1], -1),
-        (X16, BL, 2),
-        (X16, BR, -2),
-        (F16, HL, 1),
-        (F16, HR, -1),
-    ]
-
-    def halo(k, what):
-        src, dst, off = halos[k]
-        outgoing = what in ("start", "wait_send")
-        towards = off if outgoing else -off
-        there = (me < n - towards) if towards > 0 else (me >= -towards)
-
-        @pl.when(there)
-        def _():
-            copy = remote(src, dst, s_h.at[k], r_h.at[k], {"dom": lax.rem(me + off + n, n)})
-            getattr(copy, what)()
-
-    halo(0, "start")
-    halo(1, "start")
+    halo(4, "start")
+    halo(5, "start")
 
     base = diag_ref[me]
 
@@ -324,15 +351,17 @@
             value = FC[i + 1, ph, in1] + side[ph]
             X1[i + 4, ph, in1] = value
             X16[i, ph] = value.astype(bf16)
-    for k in (4, 5, 6, 7, 2, 3, 8, 9):
+    for k in range(8, 14):
         halo(k, "start")
-
-    each(n, dom_at, come1, "wait_recv")
+    for k in (6, 7):
+        halo(k, "start")
+
+    all1("wait_recv")
 
     def forward(x, before):
         value = before
         for j in range(5):
-            value = value + REC[x + 4 - j, pl.ds(2 * j, 2)]
+            value = value + REC[x + 4 - j, j]
         value = value * INV[x]
         D[x] = value
         return value
@@ -349,13 +378,13 @@
     REC2[me] = UP[pl.ds(me, 5)]
     each(n, dom_at, go2, "start")
 
-    for k in (2, 3, 8, 9):
+    for k in range(2, 8):
         halo(k, "wait_recv")
 
     def widen(p, carry):
-        for x in range(2):
+        for x in range(3):
             F[x, p, in0] = HL[x, p].astype(f32)
-            F[x + 8, p, in0] = HR[x, p].astype(f32)
+            F[x + 7, p, in0] = HR[x, p].astype(f32)
         return carry
 
     lax.fori_loop(0, 4, widen, 0)
@@ -375,14 +404,17 @@
 
     lax.fori_loop(0, 32, sweep_y, 0)
 
-    for k in (4, 5, 6, 7):
+    for k in range(8, 14):
         halo(k, "wait_recv")
+    for ph in range(2):
+        X1[2, ph, in1] = AL[ph].astype(f32)
+        X1[7, ph, in1] = AR[ph].astype(f32)
     for i in range(2):
         for ph in range(2):
             X1[i, ph, in1] = BL[i, ph].astype(f32)
             X1[i + 8, ph, in1] = BR[i, ph].astype(f32)
 
-    each(n, dom_at, come2, "wait_recv")
+    all2("wait_recv")
     for d in range(n):
         for j in range(5):
             WB[pl.ds(64 * j + 2 * d, 2)] = REC2[d, j]
@@ -481,31 +513,31 @@
     copy.wait()
 
     def panel_rows(g, carry):
-        at_o = [IDS[g, i, 0] for i in range(4)]
-        at_v = [IDS[g, i, 1] for i in range(4)]
+        at_o = [IDS[2 * g + i // 4, i % 4, 0] for i in range(8)]
+        at_v = [IDS[2 * g + i // 4, i % 4, 1] for i in range(8)]
 
         def cells(c, sums):
-            x, r = c // 8, lax.rem(c, 8) * 32
-            at = pl.ds(pl.multiple_of(r, 32), 32)
+            x, r = c // 16, lax.rem(c, 16) * 16
+            at = pl.ds(pl.multiple_of(r, 16), 16)
             pots = [pot_ref[q, x, at].astype(f32) for q in range(4)]
             new = []
-            for i in range(4):
+            for i in range(8):
                 rho = (occ[at_o[i], x, at] * vir[at_v[i], x, at]).astype(f32)
                 for q in range(4):
                     product = rho * pots[q]
-                    new.append(sums[4 * i + q] + jnp.sum(product.reshape(4, 8, 128), 0))
+                    new.append(sums[4 * i + q] + (product[:8] + product[8:]))
             return tuple(new)
 
-        sums = lax.fori_loop(0, 32, cells, tuple(jnp.zeros((8, 128), f32) for _ in range(16)))
-        for i in range(4):
+        sums = lax.fori_loop(0, 64, cells, tuple(jnp.zeros((8, 128), f32) for _ in range(32)))
+        for i in range(8):
             rows = [jnp.sum(sums[4 * i + q], 0, keepdims=True) for q in range(4)]
-            PART[4 * g + i] = jnp.concatenate(rows, 0)
-        return carry
-
-    lax.fori_loop(0, groups, panel_rows, 0)
+            PART[8 * g + i] = jnp.concatenate(rows, 0)
+        return carry
+
+    lax.fori_loop(0, groups // 2, panel_rows, 0)
     REC3[me] = PART[me]
     each(n, dom_at, go3, "start")
-    each(n, dom_at, come3, "wait_recv")
+    all3("wait_recv")
     total = lax.fori_loop(0, n, lambda s, t: t + REC3[s], jnp.zeros((4, 128), f32))
     total = jnp.concatenate([total, jnp.zeros((4, 128), f32)], 0)
     row_sums = lax.dot_general(
@@ -515,9 +547,9 @@
 
     for k in range(len(halos)):
         halo(k, "wait_send")
-    each(n, dom_at, go1, "wait_send")
-    each(n, dom_at, go2, "wait_send")
-    each(n, dom_at, go3, "wait_send")
+    all1("wait_send")
+    all2("wait_send")
+    all3("wait_send")
     each(groups, pair_at, go_id, "wait_send")
 
 
@@ -548,9 +580,12 @@
                 jax.ShapeDtypeStruct((4, 4, 256, 128), bf16),
                 jax.ShapeDtypeStruct((1, 4), f32),
             ),
-            in_specs=[pl.BlockSpec(memory_space=pltpu.SMEM)] + [whole] * 5,
+            in_specs=[pl.BlockSpec(memory_space=pl.ANY)] * 3 + [whole] * 3,
             out_specs=(whole, whole),
             scratch_shapes=[
+                vm((12, 4, 256, 128), bf16),
+                vm((12, 4, 256, 128), bf16),
+                pltpu.SMEM((4, 2), jnp.int32),
                 vm((10, 4, 272, 128), f32),
                 vm((6, 4, 272, 128), f32),
                 vm((8, 4, 272, 128), f32),
@@ -563,8 +598,8 @@
                 vm((4, 2, 128, 128), f32),
                 vm((2, 144, 128), f32),
                 vm((2, 144, 128), f32),
-                vm((n, 10, 128), f32),
-                vm((n + 4, 10, 128), f32),
+                vm((n, 5, 2, 128), f32),
+                vm((n + 4, 5, 2, 128), f32),
                 vm((n, 2, 128), f32),
                 vm((n, 2, 128), f32),
                 vm((n + 4, 2, 128), f32),
@@ -573,10 +608,12 @@
                 vm((5, 64, 128), f32),
                 vm((2, 128, 128), f32),
                 vm((2, 128, 128), f32),
-                vm((2, 4, 256, 128), bf16),
-                vm((2, 4, 256, 128), bf16),
-                vm((2, 4, 256, 128), bf16),
+                vm((4, 4, 256, 128), bf16),
+                vm((3, 4, 256, 128), bf16),
+                vm((3, 4, 256, 128), bf16),
                 vm((2, 2, 128, 128), bf16),
+                vm((2, 128, 128), bf16),
+                vm((2, 128, 128), bf16),
                 vm((2, 2, 128, 128), bf16),
                 vm((2, 2, 128, 128), bf16),
                 vm((n, 4, 128), f32),
@@ -584,9 +621,9 @@
                 vm((8, 128), jnp.int32),
                 vm((groups, 8, 128), jnp.int32),
                 pltpu.SMEM((groups, 8, 128), jnp.int32),
-                dma((n,)), dma((n,)), dma((n,)), dma((n,)), dma((n,)), dma((n,)),
+                dma(()), dma(()), dma(()), dma(()), dma(()), dma(()),
                 dma((groups,)), dma((groups,)),
-                dma((10,)), dma((10,)), dma(()),
+                dma((14,)), dma((14,)), dma(()), dma((4,)), dma((4,)), dma(()),
             ],
             compiler_params=pltpu.CompilerParams(
                 collective_id=0, has_side_effects=True, vmem_limit_bytes=56 << 20

time: 79.3 us -> 70.7 us (0.89)
  Pallas kernels: 73.7 us -> 65.1 us
    pallas_call x1, Pallas kernels: 73.7 us -> 65.1 us  [shards(): pl.pallas_call(functools.partial(kernel, n, groups), out_shape=(jax.Shape...]
where the time goes in v1:
time: 70.7 us; the launch traced here: 70.5 us
  Pallas kernels  65.1 us (92%)
  local copies, waits for them, and re-layouts  4.75 us (7%)
    pallas_call x1, Pallas kernels, shards(): pl.pallas_call(functools.partial(kernel, n, groups), out_shape=(jax.Shape...  65.1 us
    unnamed x3, local copies, waits for them, and re-layouts  4.75 us

profile of v1, /device:TPU:1, one launch (start us, length us, event | category | flops | bytes accessed | tf_op | source)
XLA Modules:
  0.0 70.5 jit_solution(17835008047173175027)
XLA Ops:
  0.6 1.3 %copy.8.ids_hbm = s32[4,2]{1,0:T(4,128)} copy(s32[4,2]{0,1:T(2,128)} %param.8) | data formatting | bytes 64 | tf_op args[2]
  2.0 65.1 %casida.1 = (bf16[4,4,256,128]{3,2,1,0:T(8,128)(2,1)}, f32[1,4]{1,0:T(1,128)}) custom-call(s32[4,2]{1,0:T(4,128)} %copy.8.ids_hbm, bf16[12,4,256,128]{3,2,1,0:T(8,128)(2,1)} %occ_hbm.1, bf16[12,4,256,128]{3,2,1,0:T(8,128)(2,1)} %vir_hbm.1, f32[64,64]{1,0:T(8,128)} %constant.6.clone.sy_ref, f32[128,128]{1,0:T(8,128)} %constant.7.clone.sz_ref, ...), custom_call_target="tpu_custom_call" | custom-call | tf_op jit(solution)/shard_map/casida/pallas_call | solution.py:577
  67.1 2.3 %copy.11 = bf16[4,4,256,128]{3,2,1,0:T(8,128)(2,1)} copy(bf16[4,4,256,128]{3,2,1,0:T(8,128)(2,1)} %get-tuple-element.4) | data formatting | bytes 2097152
  69.4 1.1 %copy.12 = f32[1,4]{1,0:T(1,128)} copy(f32[1,4]{1,0:T(1,128)} %get-tuple-element.5) | data formatting | bytes 32

commit v2 on v1

--- a/solution.py
+++ b/solution.py
@@ -125,24 +125,16 @@
     @pl.when(first)
     def _():
         HL[...] = jnp.zeros((3, 4, 256, 128), bf16)
-        AL[...] = jnp.zeros((2, 128, 128), bf16)
+        AL[...] = jnp.zeros((2, 2, 128, 128), bf16)
+        BL[...] = jnp.zeros((2, 2, 128, 128), bf16)
         CL[...] = jnp.zeros((2, 128, 128), f32)
-        X1[3] = jnp.zeros((2, 144, 128), f32)
 
     @pl.when(last)
     def _():
         HR[...] = jnp.zeros((3, 4, 256, 128), bf16)
-        AR[...] = jnp.zeros((2, 128, 128), bf16)
+        AR[...] = jnp.zeros((2, 2, 128, 128), bf16)
+        BR[...] = jnp.zeros((2, 2, 128, 128), bf16)
         CR[...] = jnp.zeros((2, 128, 128), f32)
-        X1[6] = jnp.zeros((2, 144, 128), f32)
-
-    @pl.when(me < 2)
-    def _():
-        BL[...] = jnp.zeros((2, 2, 128, 128), bf16)
-
-    @pl.when(me > n - 3)
-    def _():
-        BR[...] = jnp.zeros((2, 2, 128, 128), bf16)
 
     ids_in.wait()
 
@@ -168,7 +160,6 @@
 
         lax.fori_loop(0, 4, density, 0)
 
-    pl.semaphore_wait(barrier, n - 1 + groups - 1)
 
     def remote(src, dst, send, recv, where):
         return pltpu.make_async_remote_copy(
@@ -221,12 +212,10 @@
         (F16.at[1], HR.at[1], -1),
         (F16.at[1], HL.at[0], 1),
         (F16.at[2], HR.at[2], -1),
-        (X1.at[5, :, in1], X1.at[3, :, in1], 1),
-        (X1.at[4, :, in1], X1.at[6, :, in1], -1),
-        (X16.at[0], AL, 1),
-        (X16.at[1], AR, -1),
-        (X16, BL, 2),
-        (X16, BR, -2),
+        (X16, AL, 1),
+        (X16, AR, -1),
+        (AL, BL, 1),
+        (AR, BR, -1),
     ]
 
     def halo(k, what):
@@ -239,9 +228,6 @@
         def _():
             copy = remote(src, dst, s_h.at[k], r_h.at[k], {"dom": lax.rem(me + off + n, n)})
             getattr(copy, what)()
-
-    halo(2, "start")
-    halo(3, "start")
 
     def own_sweep(p, carry):
         for r in (0, 128):
@@ -284,8 +270,11 @@
                 value = value * mask_r
             FC[q + 1, ph, pl.ds(8, 128)] = value
 
+    pl.semaphore_wait(barrier, n - 1 + groups - 1)
     halo(0, "start")
     halo(1, "start")
+    halo(2, "start")
+    halo(3, "start")
 
     for ph in range(2):
         at = pl.ds(8, 128)
@@ -351,12 +340,14 @@
             value = FC[i + 1, ph, in1] + side[ph]
             X1[i + 4, ph, in1] = value
             X16[i, ph] = value.astype(bf16)
-    for k in range(8, 14):
+    halo(8, "start")
+    halo(9, "start")
+
+    all1("wait_recv")
+    for k in (8, 9):
+        halo(k, "wait_recv")
+    for k in (10, 11):
         halo(k, "start")
-    for k in (6, 7):
-        halo(k, "start")
-
-    all1("wait_recv")
 
     def forward(x, before):
         value = before
@@ -377,14 +368,16 @@
     lax.fori_loop(0, n, backward, jnp.zeros((2, 128), f32))
     REC2[me] = UP[pl.ds(me, 5)]
     each(n, dom_at, go2, "start")
-
-    for k in range(2, 8):
+    for k in (6, 7):
+        halo(k, "start")
+
+    for k in range(2, 6):
         halo(k, "wait_recv")
 
     def widen(p, carry):
-        for x in range(3):
+        for x in (1, 2):
             F[x, p, in0] = HL[x, p].astype(f32)
-            F[x + 7, p, in0] = HR[x, p].astype(f32)
+            F[x + 6, p, in0] = HR[x - 1, p].astype(f32)
         return carry
 
     lax.fori_loop(0, 4, widen, 0)
@@ -402,15 +395,14 @@
             Y[x + 2, p, at] = (w * (1.0 + keep)) * middle + (w * w) * sides
         return carry
 
-    lax.fori_loop(0, 32, sweep_y, 0)
-
-    for k in range(8, 14):
-        halo(k, "wait_recv")
-    for ph in range(2):
-        X1[2, ph, in1] = AL[ph].astype(f32)
-        X1[7, ph, in1] = AR[ph].astype(f32)
+    lax.fori_loop(4, 28, sweep_y, 0)
+
+    halo(10, "wait_recv")
+    halo(11, "wait_recv")
     for i in range(2):
         for ph in range(2):
+            X1[i + 2, ph, in1] = AL[i, ph].astype(f32)
+            X1[i + 6, ph, in1] = AR[i, ph].astype(f32)
             X1[i, ph, in1] = BL[i, ph].astype(f32)
             X1[i + 8, ph, in1] = BR[i, ph].astype(f32)
 
@@ -458,6 +450,18 @@
             value = keep * middle + w * (sides + X1[i + 4, ph, in1])
             V1[i + 1, ph] = value * mask1(i)
 
+    halo(6, "wait_recv")
+    halo(7, "wait_recv")
+
+    def widen_far(p, carry):
+        F[0, p, in0] = HL[0, p].astype(f32)
+        F[9, p, in0] = HR[2, p].astype(f32)
+        return carry
+
+    lax.fori_loop(0, 4, widen_far, 0)
+    lax.fori_loop(0, 4, sweep_y, 0)
+    lax.fori_loop(28, 32, sweep_y, 0)
+
     def add_coarse(j, carry):
         for p in range(4):
             for r in (0, 64):
@@ -512,31 +516,40 @@
     copy.start()
     copy.wait()
 
-    def panel_rows(g, carry):
-        at_o = [IDS[2 * g + i // 4, i % 4, 0] for i in range(8)]
-        at_v = [IDS[2 * g + i // 4, i % 4, 1] for i in range(8)]
+    def panel_rows(turn_at, carry):
+        far = 0
+        for i, offset in enumerate((4, 5, 3, 2, 6, 7, 1)):
+            far = jnp.where(turn_at == i, offset, far)
+        g = lax.rem(me // 4 + far, groups)
+        at_o = [IDS[g, i, 0] for i in range(4)]
+        at_v = [IDS[g, i, 1] for i in range(4)]
 
         def cells(c, sums):
-            x, r = c // 16, lax.rem(c, 16) * 16
-            at = pl.ds(pl.multiple_of(r, 16), 16)
+            x, r = c // 8, lax.rem(c, 8) * 32
+            at = pl.ds(pl.multiple_of(r, 32), 32)
             pots = [pot_ref[q, x, at].astype(f32) for q in range(4)]
             new = []
-            for i in range(8):
+            for i in range(4):
                 rho = (occ[at_o[i], x, at] * vir[at_v[i], x, at]).astype(f32)
                 for q in range(4):
                     product = rho * pots[q]
-                    new.append(sums[4 * i + q] + (product[:8] + product[8:]))
+                    new.append(sums[4 * i + q] + jnp.sum(product.reshape(4, 8, 128), 0))
             return tuple(new)
 
-        sums = lax.fori_loop(0, 64, cells, tuple(jnp.zeros((8, 128), f32) for _ in range(32)))
-        for i in range(8):
+        sums = lax.fori_loop(0, 32, cells, tuple(jnp.zeros((8, 128), f32) for _ in range(16)))
+        for i in range(4):
             rows = [jnp.sum(sums[4 * i + q], 0, keepdims=True) for q in range(4)]
-            PART[8 * g + i] = jnp.concatenate(rows, 0)
-        return carry
-
-    lax.fori_loop(0, groups // 2, panel_rows, 0)
+            PART[4 * g + i] = jnp.concatenate(rows, 0)
+        for i in range(4):
+
+            @pl.when(4 * g + i != me)
+            def _(i=i):
+                go3(4 * g + i).start()
+
+        return carry
+
+    lax.fori_loop(0, groups, panel_rows, 0)
     REC3[me] = PART[me]
-    each(n, dom_at, go3, "start")
     all3("wait_recv")
     total = lax.fori_loop(0, n, lambda s, t: t + REC3[s], jnp.zeros((4, 128), f32))
     total = jnp.concatenate([total, jnp.zeros((4, 128), f32)], 0)
@@ -612,8 +625,8 @@
                 vm((3, 4, 256, 128), bf16),
                 vm((3, 4, 256, 128), bf16),
                 vm((2, 2, 128, 128), bf16),
-                vm((2, 128, 128), bf16),
-                vm((2, 128, 128), bf16),
+                vm((2, 2, 128, 128), bf16),
+                vm((2, 2, 128, 128), bf16),
                 vm((2, 2, 128, 128), bf16),
                 vm((2, 2, 128, 128), bf16),
                 vm((n, 4, 128), f32),
@@ -623,7 +636,7 @@
                 pltpu.SMEM((groups, 8, 128), jnp.int32),
                 dma(()), dma(()), dma(()), dma(()), dma(()), dma(()),
                 dma((groups,)), dma((groups,)),
-                dma((14,)), dma((14,)), dma(()), dma((4,)), dma((4,)), dma(()),
+                dma((12,)), dma((12,)), dma(()), dma((4,)), dma((4,)), dma(()),
             ],
             compiler_params=pltpu.CompilerParams(
                 collective_id=0, has_side_effects=True, vmem_limit_bytes=56 << 20

time: 70.7 us -> 62.7 us (0.89)
  Pallas kernels: 65.1 us -> 57.2 us
    pallas_call x1, Pallas kernels: 65.1 us -> 57.2 us  [shards(): pl.pallas_call(functools.partial(kernel, n, groups), out_shape=(jax.Shape...]
where the time goes in v2:
time: 62.7 us; the launch traced here: 62.5 us
  Pallas kernels  57.2 us (91%)
  local copies, waits for them, and re-layouts  4.75 us (8%)
  between operations  0.64 us (1%)
    pallas_call x1, Pallas kernels, shards(): pl.pallas_call(functools.partial(kernel, n, groups), out_shape=(jax.Shape...  57.2 us
    unnamed x3, local copies, waits for them, and re-layouts  4.75 us

profile of v2, /device:TPU:1, one launch (start us, length us, event | category | flops | bytes accessed | tf_op | source)
XLA Modules:
  0.0 62.5 jit_solution(2320683311747570906)
XLA Ops:
  0.6 1.3 %copy.8.ids_hbm = s32[4,2]{1,0:T(4,128)} copy(s32[4,2]{0,1:T(2,128)} %param.8) | data formatting | bytes 64 | tf_op args[2]
  2.0 57.2 %casida.1 = (bf16[4,4,256,128]{3,2,1,0:T(8,128)(2,1)}, f32[1,4]{1,0:T(1,128)}) custom-call(s32[4,2]{1,0:T(4,128)} %copy.8.ids_hbm, bf16[12,4,256,128]{3,2,1,0:T(8,128)(2,1)} %occ_hbm.1, bf16[12,4,256,128]{3,2,1,0:T(8,128)(2,1)} %vir_hbm.1, f32[64,64]{1,0:T(8,128)} %constant.6.clone.sy_ref, f32[128,128]{1,0:T(8,128)} %constant.7.clone.sz_ref, ...), custom_call_target="tpu_custom_call" | custom-call | tf_op jit(solution)/shard_map/casida/pallas_call | solution.py:590
  59.1 2.3 %copy.11 = bf16[4,4,256,128]{3,2,1,0:T(8,128)(2,1)} copy(bf16[4,4,256,128]{3,2,1,0:T(8,128)(2,1)} %get-tuple-element.4) | data formatting | bytes 2097152
  61.4 1.1 %copy.12 = f32[1,4]{1,0:T(1,128)} copy(f32[1,4]{1,0:T(1,128)} %get-tuple-element.5) | data formatting | bytes 32

commit v3 on v2

--- a/solution.py
+++ b/solution.py
@@ -395,7 +395,7 @@
             Y[x + 2, p, at] = (w * (1.0 + keep)) * middle + (w * w) * sides
         return carry
 
-    lax.fori_loop(4, 28, sweep_y, 0)
+    lax.fori_loop(4, 28, sweep_y, 0, unroll=2)
 
     halo(10, "wait_recv")
     halo(11, "wait_recv")
@@ -497,7 +497,7 @@
             Z[x + 1, p, at] = (keep * middle + w * (sides + F[x + 3, p, at])) * mask
         return carry
 
-    lax.fori_loop(0, 24, sweep_z, 0)
+    lax.fori_loop(0, 24, sweep_z, 0, unroll=2)
 
     def sweep_out(i, carry):
         x, p = i // 4, lax.rem(i, 4)
@@ -509,7 +509,7 @@
             pot_ref[p, x, pl.ds(r, 128)] = value.astype(bf16)
         return carry
 
-    lax.fori_loop(0, 16, sweep_out, 0)
+    lax.fori_loop(0, 16, sweep_out, 0, unroll=2)
 
     each(groups, pair_at, come_id, "wait_recv")
     copy = pltpu.make_async_copy(IDR, IDS, loc)
@@ -536,7 +536,7 @@
                     new.append(sums[4 * i + q] + jnp.sum(product.reshape(4, 8, 128), 0))
             return tuple(new)
 
-        sums = lax.fori_loop(0, 32, cells, tuple(jnp.zeros((8, 128), f32) for _ in range(16)))
+        sums = lax.fori_loop(0, 32, cells, tuple(jnp.zeros((8, 128), f32) for _ in range(16)), unroll=4)
         for i in range(4):
             rows = [jnp.sum(sums[4 * i + q], 0, keepdims=True) for q in range(4)]
             PART[4 * g + i] = jnp.concatenate(rows, 0)

time: 62.7 us -> 58.5 us (0.933)
  Pallas kernels: 57.2 us -> 53 us
    pallas_call x1, Pallas kernels: 57.2 us -> 53 us  [shards(): pl.pallas_call(functools.partial(kernel, n, groups), out_shape=(jax.Shape...]
where the time goes in v3:
time: 58.5 us; the launch traced here: 58.4 us
  Pallas kernels  53 us (91%)
  local copies, waits for them, and re-layouts  4.75 us (8%)
  between operations  0.64 us (1%)
    pallas_call x1, Pallas kernels, shards(): pl.pallas_call(functools.partial(kernel, n, groups), out_shape=(jax.Shape...  53 us
    unnamed x3, local copies, waits for them, and re-layouts  4.75 us

profile of v3, /device:TPU:1, one launch (start us, length us, event | category | flops | bytes accessed | tf_op | source)
XLA Modules:
  0.0 58.4 jit_solution(13067811274799236591)
XLA Ops:
  0.6 1.3 %copy.8.ids_hbm = s32[4,2]{1,0:T(4,128)} copy(s32[4,2]{0,1:T(2,128)} %param.8) | data formatting | bytes 64 | tf_op args[2]
  2.0 53.0 %casida.1 = (bf16[4,4,256,128]{3,2,1,0:T(8,128)(2,1)}, f32[1,4]{1,0:T(1,128)}) custom-call(s32[4,2]{1,0:T(4,128)} %copy.8.ids_hbm, bf16[12,4,256,128]{3,2,1,0:T(8,128)(2,1)} %occ_hbm.1, bf16[12,4,256,128]{3,2,1,0:T(8,128)(2,1)} %vir_hbm.1, f32[64,64]{1,0:T(8,128)} %constant.6.clone.sy_ref, f32[128,128]{1,0:T(8,128)} %constant.7.clone.sz_ref, ...), custom_call_target="tpu_custom_call" | custom-call | tf_op jit(solution)/shard_map/casida/pallas_call | solution.py:590
  54.9 2.3 %copy.11 = bf16[4,4,256,128]{3,2,1,0:T(8,128)(2,1)} copy(bf16[4,4,256,128]{3,2,1,0:T(8,128)(2,1)} %get-tuple-element.4) | data formatting | bytes 2097152
  57.2 1.1 %copy.12 = f32[1,4]{1,0:T(1,128)} copy(f32[1,4]{1,0:T(1,128)} %get-tuple-element.5) | data formatting | bytes 32
